TPU v7x, 32 devices: a whole 2x2x4 slice. The times are simulated.
32 devices in a mesh: seg: 4 (over z), mem: 8 (over y, x, core).
Axes of the slice: x: 2, y: 2, z: 4, core: 2. Of those that a mesh axis runs over, the one named last changes fastest.
Arguments:
- tokens: bfloat16 [8192, 1024], P(('seg', 'mem')), may hold values from -6 to 6
- padding_mask: int32 [8192], P(('seg', 'mem')), may hold values from 0 to 1, as said below
- memory_keys: bfloat16 [4, 8192, 1024], P('seg', 'mem'), may hold values from -6 to 6
- memory_values: bfloat16 [4, 8192, 1024], P('seg', 'mem'), may hold values from -6 to 6
- memory_length: int32 [4], P('seg'), may hold values from 2048 to 8192, as said below
- chosen_keys: int32 [16, 128], P('seg'), may hold values from 0 to 8191, as said below
- norm_gain: float32 [1024], replicated, may hold values from 0.1 to 1.9
- w_query: bfloat16 [1024, 1024], replicated, may hold values from -0.1875 to 0.1875
- w_key: bfloat16 [1024, 1024], replicated, may hold values from -0.1875 to 0.1875
- w_value: bfloat16 [1024, 1024], replicated, may hold values from -0.1875 to 0.1875
- w_out: bfloat16 [1024, 1024], replicated, may hold values from -1.5 to 1.5
- ffn_gain: float32 [1024], replicated, may hold values from 0.1 to 1.9
- w_gate: bfloat16 [1024, 2816], replicated, may hold values from -0.1875 to 0.1875
- w_up: bfloat16 [1024, 2816], replicated, may hold values from -0.1875 to 0.1875
- w_down: bfloat16 [2816, 1024], replicated, may hold values from -0.109375 to 0.109375
- cotangent: bfloat16 [8192, 1024], P(('seg', 'mem')), may hold values from -6 to 6
Outputs:
- mixed: bfloat16 [8192, 1024], P(('seg', 'mem'))
- input_grad: bfloat16 [8192, 1024], P(('seg', 'mem'))
- norm_gain_grad: float32 [1024], P('mem')
- query_grad: float32 [1024, 1024], P('mem')
- key_grad: float32 [1024, 1024], P('mem')
- value_grad: float32 [1024, 1024], P('mem')
- out_grad: float32 [1024, 1024], P('mem')
- ffn_gain_grad: float32 [1024], P('mem')
- gate_grad: float32 [1024, 2816], P('mem')
- up_grad: float32 [1024, 2816], P('mem')
- down_grad: float32 [2816, 1024], P('mem')
Inputs may be any that keep to these rules, and one draw needn't show every extreme that they name: `padding_mask`: within each segment of 2048 consecutive tokens the ones form a prefix of 1024 tokens or more. `memory_length`: how many of a segment's 8192 memory slots are live. `chosen_keys`: row b belongs to the queries b * 512 to (b + 1) * 512 - 1; its first entry is below 2048.
All inputs are finite; a program needn't handle non-finite values.
Results may differ from a plain program's by a relative error of at most 0.014.
Values may be sent and summed in bfloat16 or wider, within the bound.
No kernel may reach another device: no remote copies, remote signals or barrier semaphores. Data moves between devices by JAX's collectives and lax.ppermute only.
A program may use at most 320 MiB of HBM per device.

v0:
```python
import math
import jax
import jax.numpy as jnp
from jax import lax
from jax.sharding import PartitionSpec as P

H = 8
HD = 128
SEG_LEN = 2048
QB = 512
TOPK = 128
EPSILON = 1e-05
NEGATIVE = -1e30


def outer_product(left, right):
    return lax.dot_general(
        left, right, (((0,), (0,)), ((), ())), preferred_element_type=jnp.float32
    )


def backward_dot(left, weight):
    return lax.dot_general(
        left, weight, (((1,), (1,)), ((), ())), preferred_element_type=jnp.float32
    )


def forward_dot(left, weight):
    return jnp.dot(left, weight, preferred_element_type=jnp.float32)


def normalize(values):
    factor = lax.rsqrt(jnp.mean(values * values, axis=-1, keepdims=True) + EPSILON)
    return (values * factor, factor)


def norm_back(grad_in, normed, factor, gain):
    scaled = grad_in * gain
    return factor * (scaled - normed * jnp.mean(scaled * normed, axis=-1, keepdims=True))


def block_stats(scores, usable):
    highest = jnp.max(scores, axis=-1)
    row_sum = jnp.sum(jnp.where(usable, jnp.exp(scores - highest[..., None]), 0.0), axis=-1)
    return (highest, row_sum)


def join_stats(high_left, sum_left, high_right, sum_right):
    highest = jnp.maximum(high_left, high_right)
    return (
        highest,
        sum_left * jnp.exp(high_left - highest) + sum_right * jnp.exp(high_right - highest),
    )


def local(
    tokens,
    padding_mask,
    memory_keys,
    memory_values,
    memory_length,
    chosen_keys,
    norm_gain,
    w_query,
    w_key,
    w_value,
    w_out,
    ffn_gain,
    w_gate,
    w_up,
    w_down,
    cotangent,
):
    group_size = lax.axis_size("mem")
    position = lax.axis_index("mem")
    tok_rows, model_width = tokens.shape
    memory_rows = memory_keys.shape[1]
    segment_count = memory_keys.shape[0]
    all_rows = tok_rows * group_size
    blocks = all_rows // QB
    segment_blocks = SEG_LEN // QB
    score_scale = 1.0 / math.sqrt(HD)
    inputs = tokens.astype(jnp.float32)
    normed_one, factor_one = normalize(inputs)
    h_one = (normed_one * norm_gain).astype(jnp.bfloat16)
    queries = forward_dot(h_one, w_query).astype(jnp.bfloat16)
    keyed_flat = forward_dot(h_one, w_key).astype(jnp.bfloat16)
    valued_flat = forward_dot(h_one, w_value).astype(jnp.bfloat16)
    own_keys = keyed_flat.reshape(tok_rows, H, HD)
    own_values = valued_flat.reshape(tok_rows, H, HD)
    first_row = position * tok_rows
    own_segment = first_row // SEG_LEN
    own_offset = first_row % SEG_LEN
    start_block = own_segment * segment_blocks
    key_position = own_offset + jnp.arange(tok_rows)
    key_usable = padding_mask == 1
    block_segment = jnp.arange(blocks) * QB // SEG_LEN
    segment_match = block_segment[:, None] == jnp.arange(segment_count)[None, :]
    limits = jnp.sum(jnp.where(segment_match, memory_length[None, :], 0), axis=1)
    shifted = chosen_keys - position * memory_rows
    owned = (shifted >= 0) & (shifted < memory_rows) & (chosen_keys < limits[:, None])
    columns = jnp.arange(memory_rows)

    def select_slots(pieces):
        local_rows, usable, segment = pieces
        table = ((local_rows[:, None] == columns[None, :]) & usable[:, None]).astype(jnp.bfloat16)
        keys_here = lax.dynamic_index_in_dim(memory_keys, segment, 0, keepdims=False)
        values_here = lax.dynamic_index_in_dim(memory_values, segment, 0, keepdims=False)
        return (
            forward_dot(table, keys_here).astype(jnp.bfloat16),
            forward_dot(table, values_here).astype(jnp.bfloat16),
        )

    picked_keys, picked_values = lax.map(select_slots, (shifted, owned, block_segment))
    gathered = lax.all_gather(queries, "mem", axis=0, tiled=True).reshape(blocks, QB, H, HD)
    picked_keys = picked_keys.reshape(blocks, TOPK, H, HD)
    picked_values = picked_values.reshape(blocks, TOPK, H, HD)

    def memory_scores(query_block, key_block, usable):
        scores = (
            jnp.einsum("qhd,thd->qht", query_block, key_block, preferred_element_type=jnp.float32)
            * score_scale
        )
        return jnp.where(usable[None, None, :], scores, NEGATIVE)

    def local_visible(block_index):
        query_position = block_index * QB + jnp.arange(QB)
        return (key_position[None, :] <= query_position[:, None]) & key_usable[None, :]

    def local_scores(query_block, visible):
        scores = (
            jnp.einsum("qhd,khd->qhk", query_block, own_keys, preferred_element_type=jnp.float32)
            * score_scale
        )
        return jnp.where(visible[:, None, :], scores, NEGATIVE)

    def segment_rows(source, block_index):
        return lax.dynamic_index_in_dim(source, start_block + block_index, 0, keepdims=False)

    def add_segment(whole, local_part):
        merged = lax.dynamic_slice_in_dim(whole, start_block, segment_blocks, 0) + local_part
        return lax.dynamic_update_slice_in_dim(whole, merged, start_block, 0)

    def memory_first(pieces):
        query_block, key_block, usable = pieces
        return block_stats(memory_scores(query_block, key_block, usable), usable[None, None, :])

    memory_high, memory_sum = lax.map(memory_first, (gathered, picked_keys, owned))

    def local_first(block_index):
        visible = local_visible(block_index)
        scores = local_scores(segment_rows(gathered, block_index), visible)
        return block_stats(scores, visible[:, None, :])

    local_high, local_sum = lax.map(local_first, jnp.arange(segment_blocks))
    seg_high = lax.dynamic_slice_in_dim(memory_high, start_block, segment_blocks, 0)
    seg_sum = lax.dynamic_slice_in_dim(memory_sum, start_block, segment_blocks, 0)
    seg_high, seg_sum = join_stats(seg_high, seg_sum, local_high, local_sum)
    memory_high = lax.dynamic_update_slice_in_dim(memory_high, seg_high, start_block, 0)
    memory_sum = lax.dynamic_update_slice_in_dim(memory_sum, seg_sum, start_block, 0)
    row_high = lax.pmax(memory_high.astype(jnp.bfloat16), "mem").astype(memory_high.dtype)
    row_sum = lax.psum(memory_sum * jnp.exp(memory_high - row_high), "mem")
    log_total = row_high + jnp.log(row_sum)

    def memory_second(pieces):
        query_block, key_block, value_block, usable, block_total = pieces
        scores = memory_scores(query_block, key_block, usable)
        weights = jnp.where(
            usable[None, None, :], jnp.exp(scores - block_total[..., None]), 0.0
        ).astype(jnp.bfloat16)
        return jnp.einsum("qht,thd->qhd", weights, value_block, preferred_element_type=jnp.float32)

    numerators = lax.map(memory_second, (gathered, picked_keys, picked_values, owned, log_total))

    def local_second(block_index):
        visible = local_visible(block_index)
        scores = local_scores(segment_rows(gathered, block_index), visible)
        block_total = segment_rows(log_total, block_index)
        weights = jnp.where(
            visible[:, None, :], jnp.exp(scores - block_total[..., None]), 0.0
        ).astype(jnp.bfloat16)
        return jnp.einsum("qhk,khd->qhd", weights, own_values, preferred_element_type=jnp.float32)

    numerators = add_segment(numerators, lax.map(local_second, jnp.arange(segment_blocks)))
    attended_sum = lax.psum_scatter(
        numerators.reshape(all_rows, model_width), "mem", scatter_dimension=0, tiled=True
    )
    attended = attended_sum.astype(jnp.bfloat16)
    residual = inputs + forward_dot(attended, w_out)
    normed_two, factor_two = normalize(residual)
    h_two = (normed_two * ffn_gain).astype(jnp.bfloat16)
    gate = forward_dot(h_two, w_gate)
    up_part = forward_dot(h_two, w_up)
    sigmoid_gate = jax.nn.sigmoid(gate)
    silu_gate = gate * sigmoid_gate
    act = (silu_gate * up_part).astype(jnp.bfloat16)
    mixed = (residual + forward_dot(act, w_down)).astype(jnp.bfloat16)
    down_grad = outer_product(act, cotangent)
    d_act = backward_dot(cotangent, w_down)
    d_gate = (d_act * up_part * sigmoid_gate * (1.0 + gate * (1.0 - sigmoid_gate))).astype(
        jnp.bfloat16
    )
    d_up = (d_act * silu_gate).astype(jnp.bfloat16)
    gate_grad = outer_product(h_two, d_gate)
    up_grad = outer_product(h_two, d_up)
    d_two = backward_dot(d_gate, w_gate) + backward_dot(d_up, w_up)
    ffn_gain_grad = jnp.sum(d_two * normed_two, axis=0)
    d_res = cotangent.astype(jnp.float32) + norm_back(d_two, normed_two, factor_two, ffn_gain)
    d_res_low = d_res.astype(jnp.bfloat16)
    out_grad = outer_product(attended, d_res_low)
    d_att = backward_dot(d_res_low, w_out).astype(jnp.bfloat16)
    grad_rows = lax.all_gather(d_att, "mem", axis=0, tiled=True).reshape(blocks, QB, H, HD)

    def memory_third(pieces):
        query_block, key_block, value_block, usable, block_total, grad_block = pieces
        scores = memory_scores(query_block, key_block, usable)
        probs = jnp.where(usable[None, None, :], jnp.exp(scores - block_total[..., None]), 0.0)
        pushes = jnp.einsum(
            "qhd,thd->qht", grad_block, value_block, preferred_element_type=jnp.float32
        )
        return jnp.sum(probs * pushes, axis=-1)

    delta_part = lax.map(
        memory_third, (gathered, picked_keys, picked_values, owned, log_total, grad_rows)
    )

    def local_third(block_index):
        visible = local_visible(block_index)
        scores = local_scores(segment_rows(gathered, block_index), visible)
        block_total = segment_rows(log_total, block_index)
        probs = jnp.where(visible[:, None, :], jnp.exp(scores - block_total[..., None]), 0.0)
        pushes = jnp.einsum(
            "qhd,khd->qhk",
            segment_rows(grad_rows, block_index),
            own_values,
            preferred_element_type=jnp.float32,
        )
        return jnp.sum(probs * pushes, axis=-1)

    delta_part = add_segment(delta_part, lax.map(local_third, jnp.arange(segment_blocks)))
    delta = lax.psum(delta_part, "mem")

    def memory_fourth(pieces):
        query_block, key_block, value_block, usable, block_total, grad_block, block_delta = pieces
        scores = memory_scores(query_block, key_block, usable)
        probs = jnp.where(usable[None, None, :], jnp.exp(scores - block_total[..., None]), 0.0)
        pushes = jnp.einsum(
            "qhd,thd->qht", grad_block, value_block, preferred_element_type=jnp.float32
        )
        d_scores = jnp.where(
            usable[None, None, :], probs * (pushes - block_delta[..., None]), 0.0
        ).astype(jnp.bfloat16)
        return (
            jnp.einsum("qht,thd->qhd", d_scores, key_block, preferred_element_type=jnp.float32)
            * score_scale
        )

    query_terms = lax.map(
        memory_fourth, (gathered, picked_keys, picked_values, owned, log_total, grad_rows, delta)
    )

    def local_fourth(running, block_index):
        key_acc, value_acc = running
        visible = local_visible(block_index)
        query_block = segment_rows(gathered, block_index)
        grad_block = segment_rows(grad_rows, block_index)
        scores = local_scores(query_block, visible)
        block_total = segment_rows(log_total, block_index)
        block_delta = segment_rows(delta, block_index)
        probs = jnp.where(visible[:, None, :], jnp.exp(scores - block_total[..., None]), 0.0)
        pushes = jnp.einsum(
            "qhd,khd->qhk", grad_block, own_values, preferred_element_type=jnp.float32
        )
        d_scores = jnp.where(
            visible[:, None, :], probs * (pushes - block_delta[..., None]), 0.0
        ).astype(jnp.bfloat16)
        query_term = (
            jnp.einsum("qhk,khd->qhd", d_scores, own_keys, preferred_element_type=jnp.float32)
            * score_scale
        )
        key_acc = (
            key_acc
            + jnp.einsum("qhk,qhd->khd", d_scores, query_block, preferred_element_type=jnp.float32)
            * score_scale
        )
        value_acc = value_acc + jnp.einsum(
            "qhk,qhd->khd",
            probs.astype(jnp.bfloat16),
            grad_block,
            preferred_element_type=jnp.float32,
        )
        return ((key_acc, value_acc), query_term)

    empty_acc = jnp.zeros((tok_rows, H, HD), jnp.float32)
    (key_sum, value_sum), local_terms = lax.scan(
        local_fourth, (empty_acc, empty_acc), jnp.arange(segment_blocks)
    )
    query_terms = add_segment(query_terms, local_terms)
    d_query = lax.psum_scatter(
        query_terms.reshape(all_rows, model_width), "mem", scatter_dimension=0, tiled=True
    ).astype(jnp.bfloat16)
    d_key = key_sum.reshape(tok_rows, model_width).astype(jnp.bfloat16)
    d_value = value_sum.reshape(tok_rows, model_width).astype(jnp.bfloat16)
    query_grad = outer_product(h_one, d_query)
    key_grad = outer_product(h_one, d_key)
    value_grad = outer_product(h_one, d_value)
    d_one = (
        backward_dot(d_query, w_query) + backward_dot(d_key, w_key) + backward_dot(d_value, w_value)
    )
    norm_gain_grad = jnp.sum(d_one * normed_one, axis=0)
    input_grad = (d_res + norm_back(d_one, normed_one, factor_one, norm_gain)).astype(jnp.bfloat16)
    shards = (
        lax.psum_scatter(norm_gain_grad, "mem", scatter_dimension=0, tiled=True),
        lax.psum_scatter(query_grad, "mem", scatter_dimension=0, tiled=True),
        lax.psum_scatter(key_grad, "mem", scatter_dimension=0, tiled=True),
        lax.psum_scatter(value_grad, "mem", scatter_dimension=0, tiled=True),
        lax.psum_scatter(out_grad, "mem", scatter_dimension=0, tiled=True),
        lax.psum_scatter(ffn_gain_grad, "mem", scatter_dimension=0, tiled=True),
        lax.psum_scatter(gate_grad, "mem", scatter_dimension=0, tiled=True),
        lax.psum_scatter(up_grad, "mem", scatter_dimension=0, tiled=True),
        lax.psum_scatter(down_grad, "mem", scatter_dimension=0, tiled=True),
    )
    (
        norm_part,
        query_part,
        key_part,
        value_part,
        out_part,
        ffn_gain_part,
        gate_part,
        up_grad_part,
        down_part,
    ) = shards
    summed = lax.psum(
        (
            norm_part,
            query_part,
            key_part,
            value_part,
            out_part,
            ffn_gain_part,
            gate_part,
            up_grad_part,
            down_part,
        ),
        "seg",
    )
    (
        norm_done,
        query_done,
        key_done,
        value_done,
        out_done,
        ffn_gain_done,
        gate_done,
        up_done,
        down_done,
    ) = summed
    return (
        mixed,
        input_grad,
        norm_done,
        query_done,
        key_done,
        value_done,
        out_done,
        ffn_gain_done,
        gate_done,
        up_done,
        down_done,
    )


def solution(mesh):
    return jax.shard_map(
        local,
        mesh=mesh,
        in_specs=(
            P(("seg", "mem"), None),
            P(("seg", "mem")),
            P("seg", "mem", None),
            P("seg", "mem", None),
            P("seg"),
            P("seg", None),
            P(),
            P(),
            P(),
            P(),
            P(),
            P(),
            P(),
            P(),
            P(),
            P(("seg", "mem"), None),
        ),
        out_specs=(
            P(("seg", "mem"), None),
            P(("seg", "mem"), None),
            P("mem"),
            P("mem", None),
            P("mem", None),
            P("mem", None),
            P("mem", None),
            P("mem"),
            P("mem", None),
            P("mem", None),
            P("mem", None),
        ),
        check_vma=False,
    )
```

profile of v0, /device:TPU:0, one launch (start us, length us, event | category | flops | bytes accessed | tf_op | source)
XLA Modules:
  0.0 1458.7 jit_solution(2463133091801142676)
XLA Ops:
  15.4 22.5 %while.110 = (s32[]{:T(128)}, bf16[4,128,1024]{2,1,0:T(8,128)(2,1)}, bf16[4,128,1024]{2,1,0:T(8,128)(2,1)}, s32[4,128]{1,0:T(4,128)S(1)}, pred[4,128]{1,0:T(4,12...) while((s32[]{:T(128)}, bf16[4,128,1024]{2,1,0:T(8,128)(2,1)}, ...), condition=%wide.region_2.3_spmd.clone, body=%wide.region_1.2_spmd.clone.sunk | while | flops 537657344 | bytes 4721261 | solution.py:114
  40.4 11.2 all-gather.3.cloned.1.call-done
  57.8 20.9 %while.111 = (s32[]{:T(128)}, f32[4,512,8]{1,2,0:T(8,128)S(1)}, f32[4,512,8]{1,2,0:T(8,128)S(1)}, s32[4]{0:T(128)S(1)}, pred[256]{0:T(512)(128)(4,1)S(1)}, /*ind...) while((s32[]{:T(128)}, f32[4,512,8]{1,2,0:T(8,128)S(1)}, ...), condition=%wide.region_10.11_spmd.clone, body=%wide.region_7.10_spmd.clone.sunk | while | flops 277078784 | bytes 10475995 | solution.py:155
  78.8 9.8 while.106
  88.6 23.5 %pmax.7 = bf16[4,512,8]{1,2,0:T(8,128)(2,1)S(1)} all-reduce(bf16[4,512,8]{1,2,0:T(8,128)(2,1)S(1)} %get-tuple-element.1010), channel_id=1, replica_groups=mesh['seg'=4,'mem'=8] {'mem'}, use_global_device_ids=true, to_apply=%region_11.12 | all-reduce | flops 16384 | bytes 65536 | tf_op jit(solution)/shard_map/pmax | solution.py:161
  119.1 46.3 %all-reduce.9.cloned.1.call-done = f32[4,512,8]{1,2,0:T(8,128)} async-done(((f32[4,512,8]{1,2,0:T(8,128)}), f32[4,512,8]{1,2,0:T(8,128)}) %all-reduce.9.cloned.1.call-update) | async-done | bytes 65552 | tf_op jit(solution)/shard_map/psum | solution.py:162
  166.3 4.2 broadcast.311.clone3.1
  170.5 26.2 %while.112 = (s32[]{:T(128)}, f32[4,512,8,128]{3,1,2,0:T(8,128)}, s32[4]{0:T(128)S(1)}, pred[256]{0:T(512)(128)(4,1)S(1)}, s32[]{:T(128)}, /*index=5*/bf16[4,512...) while((s32[]{:T(128)}, f32[4,512,8,128]{3,1,2,0:T(8,128)}, ...), condition=%wide.region_16.17_spmd.clone, body=%wide.region_15.16_spmd.clone.sunk | while | flops 542376704 | bytes 4643303 | solution.py:184
  172.6 4.4 bitcast_dynamic-update-slice_fusion.17
  179.2 4.4 bitcast_dynamic-update-slice_fusion.17
  185.7 4.5 bitcast_dynamic-update-slice_fusion.17
  192.3 4.5 bitcast_dynamic-update-slice_fusion.17
  201.0 46.6 %while.107 = (s32[]{:T(128)}, f32[4,512,8,128]{3,1,2,0:T(8,128)}, bf16[4,128,8,128]{3,2,1,0:T(8,128)(2,1)}, pred[4,128]{1,0:T(4,128)(4,1)S(1)}, bf16[4,128,8,128...) while((s32[]{:T(128)}, f32[4,512,8,128]{3,1,2,0:T(8,128)}, ...), condition=%wide.region_14.15_spmd, body=%wide.region_13.14_spmd.sunk | while | flops 271056896 | bytes 13158765 | solution.py:173
  247.5 10.3 add.250
  257.8 8.2 copy.98
  266.1 5.3 copy.150
  271.5 70.8 %reduce-scatter.10.cloned.1.call-done = f32[256,1024]{1,0:T(8,128)} async-done(((f32[2048,1024]{1,0:T(8,128)}), f32[256,1024]{1,0:T(8,128)}) %reduce-scatter.10.cloned.1.call-update) | async-done | bytes 1048592 | tf_op jit(solution)/shard_map/reduce_scatter | solution.py:185
  345.4 6.3 fusion.216
  355.0 5.9 multiply_convert_fusion
  370.4 34.3 %all-gather.5.cloned.1.call-done = bf16[2048,1024]{1,0:T(8,128)(2,1)} async-done(((bf16[256,1024]{1,0:T(8,128)(2,1)}), bf16[2048,1024]{1,0:T(8,128)(2,1)}) %all-gather.5.cloned.1.call-update) | async-done | bytes 4194320 | tf_op jit(solution)/shard_map/all_gather | solution.py:212
  410.9 28.1 %while.113 = (s32[]{:T(128)}, f32[4,512,8]{1,2,0:T(8,128)S(1)}, s32[4]{0:T(128)S(1)}, pred[256]{0:T(512)(128)(4,1)S(1)}, s32[]{:T(128)}, /*index=5*/bf16[4,512,8...) while((s32[]{:T(128)}, f32[4,512,8]{1,2,0:T(8,128)S(1)}, ...), condition=%wide.region_25.26_spmd.clone, body=%wide.region_23.25_spmd.clone.sunk | while | flops 543421184 | bytes 12032499 | solution.py:240
  439.0 15.7 %while.108 = (s32[]{:T(128)}, f32[4,512,8]{1,2,0:T(8,128)S(1)}, pred[4,128]{1,0:T(4,128)(4,1)S(1)}, bf16[4,128,8,128]{3,1,2,0:T(8,128)(2,1)}, bf16[4,512,8,128]{...) while((s32[]{:T(128)}, f32[4,512,8]{1,2,0:T(8,128)S(1)}, ...), condition=%wide.region_22.23_spmd, body=%wide.region_20.22_spmd.sunk | while | flops 271577088 | bytes 6917489 | solution.py:223
  455.5 52.6 %all-reduce.11.cloned.1.call-done = f32[4,512,8]{1,2,0:T(8,128)} async-done(((f32[4,512,8]{1,2,0:T(8,128)}), f32[4,512,8]{1,2,0:T(8,128)}) %all-reduce.11.cloned.1.call-update) | async-done | bytes 65552 | tf_op jit(solution)/shard_map/psum | solution.py:241
  512.3 55.4 %while.109 = (s32[]{:T(128)}, f32[4,512,8,128]{3,1,2,0:T(8,128)}, bf16[4,128,8,128]{3,1,2,0:T(8,128)(2,1)}, pred[4,128]{1,0:T(4,128)(4,1)S(1)}, bf16[4,512,8,128...) while((s32[]{:T(128)}, f32[4,512,8,128]{3,1,2,0:T(8,128)}, ...), condition=%wide.region_28.29_spmd, body=%wide.region_27.28_spmd.sunk | while | flops 407371776 | bytes 17665912 | solution.py:258
  515.6 4.6 multiply_bitcast_fusion.2
  529.4 4.6 multiply_bitcast_fusion.2
  543.3 4.6 multiply_bitcast_fusion.2
  557.0 4.6 multiply_bitcast_fusion.2
  571.9 50.7 %while.114 = (s32[]{:T(128)}, f32[256,8,128]{0,2,1:T(8,128)}, f32[256,8,128]{0,2,1:T(8,128)}, f32[4,512,8,128]{3,1,2,0:T(8,128)}, s32[4]{0:T(128)S(1)}, /*index=...) while((s32[]{:T(128)}, f32[256,8,128]{0,2,1:T(8,128)}, ...), condition=%wide.region_30.31_spmd.clone, body=%wide.region_29.30_spmd.clone.sunk | while | flops 1357906688 | bytes 65264296 | solution.py:295
  622.6 10.3 add.259
  632.9 8.2 copy.117
  641.1 5.4 copy.149
  646.6 4.4 fusion.199
  661.5 7.7 fusion.219
  669.2 7.4 fusion.218
  676.7 7.6 fusion.220
  684.4 33.0 %reduce-scatter.12.cloned.1.call-done = f32[256,1024]{1,0:T(8,128)} async-done(((f32[2048,1024]{1,0:T(8,128)}), f32[256,1024]{1,0:T(8,128)}) %reduce-scatter.12.cloned.1.call-update) | async-done | bytes 1048592 | tf_op jit(solution)/shard_map/reduce_scatter | solution.py:299
  721.5 50.6 %reduce-scatter.20.cloned.1.call-done = f32[128,1024]{1,0:T(8,128)} async-done(((f32[1024,1024]{1,0:T(8,128)}), f32[128,1024]{1,0:T(8,128)}) %reduce-scatter.20.cloned.1.call-update) | async-done | bytes 524304 | tf_op jit(solution)/shard_map/reduce_scatter | solution.py:317
  772.1 55.1 %reduce-scatter.18.cloned.1.call-done = f32[128,1024]{1,0:T(8,128)} async-done(((f32[1024,1024]{1,0:T(8,128)}), f32[128,1024]{1,0:T(8,128)}) %reduce-scatter.18.cloned.1.call-update) | async-done | bytes 524304 | tf_op jit(solution)/shard_map/reduce_scatter | solution.py:316
  827.2 54.7 %reduce-scatter.16.cloned.1.call-done = f32[128,1024]{1,0:T(8,128)} async-done(((f32[1024,1024]{1,0:T(8,128)}), f32[128,1024]{1,0:T(8,128)}) %reduce-scatter.16.cloned.1.call-update) | async-done | bytes 524304 | tf_op jit(solution)/shard_map/reduce_scatter | solution.py:315
  881.9 90.6 %reduce-scatter.24.cloned.1.call-done = f32[128,2816]{1,0:T(8,128)} async-done(((f32[1024,2816]{1,0:T(8,128)}), f32[128,2816]{1,0:T(8,128)}) %reduce-scatter.24.cloned.1.call-update) | async-done | bytes 1441808 | tf_op jit(solution)/shard_map/reduce_scatter | solution.py:320
  972.4 90.7 %reduce-scatter.22.cloned.1.call-done = f32[128,2816]{1,0:T(8,128)} async-done(((f32[1024,2816]{1,0:T(8,128)}), f32[128,2816]{1,0:T(8,128)}) %reduce-scatter.22.cloned.1.call-update) | async-done | bytes 1441808 | tf_op jit(solution)/shard_map/reduce_scatter | solution.py:319
  1063.1 90.5 %reduce-scatter.26.cloned.1.call-done = f32[352,1024]{1,0:T(8,128)} async-done(((f32[2816,1024]{1,0:T(8,128)}), f32[352,1024]{1,0:T(8,128)}) %reduce-scatter.26.cloned.1.call-update) | async-done | bytes 1441808 | tf_op jit(solution)/shard_map/reduce_scatter | solution.py:321
  1153.7 55.0 %reduce-scatter.14.cloned.1.call-done = f32[128,1024]{1,0:T(8,128)} async-done(((f32[1024,1024]{1,0:T(8,128)}), f32[128,1024]{1,0:T(8,128)}) %reduce-scatter.14.cloned.1.call-update) | async-done | bytes 524304 | tf_op jit(solution)/shard_map/reduce_scatter | solution.py:314
  1210.0 5.9 fusion.184
  1221.0 13.1 all-reduce.2
  1234.3 12.5 all-reduce.3
  1249.5 191.5 %all-reduce.13.cloned.1.call-done = (f32[128,1024]{1,0:T(8,128)}, f32[128,1024]{1,0:T(8,128)}, f32[128,1024]{1,0:T(8,128)}, f32[128,1024]{1,0:T(8,128)}, f32[128...) async-done(((f32[128,1024]{1,0:T(8,128)}, f32[128,1024]{1,0:T(8,128)}, f32[128,1024]{1,0:T(8,128)}, f32[128,1024]{1,0:T(8,128)}, f32[128,2816]{1,0:T(8,128)}, ...) | async-done | bytes 6422544 | tf_op jit(solution)/shard_map/psum | solution.py:334
  (429 shorter events, 309.7 us)
Async XLA Ops:
  7.2 106.0 %copy-start = (bf16[1024,1024]{1,0:T(8,128)(2,1)S(1)}, bf16[1024,1024]{1,0:T(8,128)(2,1)}, u32[]{:S(2)}) copy-start(bf16[1024,1024]{1,0:T(8,128)(2,1)} %param.43) | copy-start | bytes 6291460
  7.2 5.6 copy-start.3
  7.2 5.6 copy-start.25
  7.2 44.4 %all-gather.3.cloned.1.call-start = ((), (), s32[]{:S(2)}) async-start(), calls=%async_computation.9 | async-start | bytes 4718592 | tf_op jit(solution)/shard_map/all_gather | solution.py:115
  8.6 104.5 %copy-start.27 = (f32[256]{0:T(256)}, f32[256]{0:T(256)S(1)}, u32[]{:S(2)}) copy-start(f32[256]{0:T(256)S(1)} %add_rsqrt_fusion.1) | copy-start | bytes 3076
  8.7 6.6 copy-start.32
  8.7 6.7 copy-start.30
  12.1 153.4 %all-reduce.9.cloned.1.call-start = ((), (), s32[]{:S(2)}) async-start(), calls=%async_computation.10 | async-start | bytes 131072 | tf_op jit(solution)/shard_map/psum | solution.py:162
  112.8 229.5 %reduce-scatter.10.cloned.1.call-start = ((), (), s32[]{:S(2)}) async-start(), calls=%async_computation.11 | async-start | bytes 9437184 | tf_op jit(solution)/shard_map/reduce_scatter | solution.py:185
  271.5 73.7 %copy-start.29 = (f32[1024]{0:T(1024)S(1)}, f32[1024]{0:T(1024)}, u32[]{:S(2)}) copy-start(f32[1024]{0:T(1024)} %param.45) | copy-start | bytes 12292
  271.5 133.3 %all-gather.5.cloned.1.call-start = ((), (), s32[]{:S(2)}) async-start(), calls=%async_computation.12 | async-start | bytes 4718592 | tf_op jit(solution)/shard_map/all_gather | solution.py:212
  342.3 9.4 slice-start
  345.1 19.9 %copy-start.6 = (f32[256,1024]{1,0:T(8,128)}, f32[256,1024]{1,0:T(8,128)S(1)}, u32[]{:S(2)}) copy-start(f32[256,1024]{1,0:T(8,128)S(1)} %get-tuple-element.1028) | copy-start | bytes 3145732
  345.3 6.3 copy-start.10
  345.3 6.3 slice-start.1
  345.4 9.6 slice-start.4
  351.7 3.3 copy-start.15
  351.7 3.3 slice-start.5
  351.7 10.9 slice-start.2
  355.0 7.6 slice-start.3
  362.6 3.7 copy-start.7
  367.9 140.2 %all-reduce.11.cloned.1.call-start = ((), (), s32[]{:S(2)}) async-start(), calls=%async_computation.13 | async-start | bytes 131072 | tf_op jit(solution)/shard_map/psum | solution.py:241
  408.0 2.9 copy-start.23
  455.4 261.9 %reduce-scatter.12.cloned.1.call-start = ((), (), s32[]{:S(2)}) async-start(), calls=%async_computation.14 | async-start | bytes 9437184 | tf_op jit(solution)/shard_map/reduce_scatter | solution.py:299
  508.0 4.2 copy-start.24
  573.8 2.5 copy-start.11
  573.8 2.8 copy-start.21
  586.3 2.5 copy-start.11
  586.4 2.8 copy-start.21
  598.9 2.5 copy-start.11
  598.9 2.8 copy-start.21
  611.5 2.5 copy-start.11
  611.5 2.8 copy-start.21
  646.5 125.5 %reduce-scatter.20.cloned.1.call-start = ((), (), s32[]{:S(2)}) async-start(), calls=%async_computation.18 | async-start | bytes 4718592 | tf_op jit(solution)/shard_map/reduce_scatter | solution.py:317
  651.0 176.2 %reduce-scatter.18.cloned.1.call-start = ((), (), s32[]{:S(2)}) async-start(), calls=%async_computation.17 | async-start | bytes 4718592 | tf_op jit(solution)/shard_map/reduce_scatter | solution.py:316
  655.9 226.0 %reduce-scatter.16.cloned.1.call-start = ((), (), s32[]{:S(2)}) async-start(), calls=%async_computation.16 | async-start | bytes 4718592 | tf_op jit(solution)/shard_map/reduce_scatter | solution.py:315
  661.2 311.2 %reduce-scatter.24.cloned.1.call-start = ((), (), s32[]{:S(2)}) async-start(), calls=%async_computation.20 | async-start | bytes 12976128 | tf_op jit(solution)/shard_map/reduce_scatter | solution.py:320
  669.1 394.0 %reduce-scatter.22.cloned.1.call-start = ((), (), s32[]{:S(2)}) async-start(), calls=%async_computation.19 | async-start | bytes 12976128 | tf_op jit(solution)/shard_map/reduce_scatter | solution.py:319
  676.7 477.0 %reduce-scatter.26.cloned.1.call-start = ((), (), s32[]{:S(2)}) async-start(), calls=%async_computation.21 | async-start | bytes 12976128 | tf_op jit(solution)/shard_map/reduce_scatter | solution.py:321
  684.3 524.4 %reduce-scatter.14.cloned.1.call-start = ((), (), s32[]{:S(2)}) async-start(), calls=%async_computation.15 | async-start | bytes 4718592 | tf_op jit(solution)/shard_map/reduce_scatter | solution.py:314
  721.4 487.3 %copy-start.33 = (u32[32]{0:T(128)S(1)}, u32[32]{0:T(128)}, u32[]{:S(2)}) copy-start(u32[32]{0:T(128)} %constant.261) | copy-start | bytes 388
  721.4 719.5 %all-reduce.13.cloned.1.call-start = ((), (), s32[]{:S(2)}) async-start(), calls=%async_computation.22 | async-start | bytes 12845056 | tf_op jit(solution)/shard_map/psum | solution.py:334
  1210.0 5.9 copy-start.12
  1210.0 5.9 copy-start.13
  1218.4 2.7 copy-start.31
  1440.9 7.8 copy-start.20
  1440.9 8.9 copy-start.19
  1443.0 8.0 copy-start.18
  (21 other events, 39.3 us)
Sparse Core Ops, SparseCore 0:
  12.2 39.4 all-gather.2
  112.9 52.4 all-reduce.8
  271.6 70.6 reduce-scatter.9
  368.0 36.7 all-gather.4
  455.5 52.4 all-reduce.10
  646.7 70.6 reduce-scatter.11
  720.7 51.3 reduce-scatter.19
  775.8 51.3 reduce-scatter.17
  830.5 51.2 reduce-scatter.15
  885.6 86.7 reduce-scatter.23
  976.3 86.7 reduce-scatter.21
  1066.9 86.7 reduce-scatter.25
  1157.4 51.2 reduce-scatter.13
  1211.5 229.3 all-reduce.12
where the time goes:
time: 1470 us; the launch traced here: 1460 us
  waiting for transfers between devices  927 us (63%)
  matrix products  254 us (17%)
  local copies, waits for them, and re-layouts  149 us (10%)
  blocking collectives  49.1 us (3%)
  other arithmetic  39.6 us (3%)
  loops' own time  23.4 us (2%)
  between operations  16.1 us (1%)
    psum x1, waiting for transfers between devices, local(): lax.psum((norm_part, query_part, key_part, value_part, out_part, ffn_gain...  191 us
    reduce_scatter x1, waiting for transfers between devices, local(): lax.psum_scatter(gate_grad, 'mem', scatter_dimension=0, tiled=True)  90.7 us
    reduce_scatter x1, waiting for transfers between devices, local(): lax.psum_scatter(up_grad, 'mem', scatter_dimension=0, tiled=True)  90.6 us
    reduce_scatter x1, waiting for transfers between devices, local(): lax.psum_scatter(down_grad, 'mem', scatter_dimension=0, tiled=True)  90.5 us
    reduce_scatter x1, waiting for transfers between devices, local(): lax.psum_scatter(numerators.reshape(all_rows, model_width), 'mem', scatte...  70.8 us
    reduce_scatter x1, waiting for transfers between devices, local(): lax.psum_scatter(value_grad, 'mem', scatter_dimension=0, tiled=True)  55.1 us
    reduce_scatter x1, waiting for transfers between devices, local(): lax.psum_scatter(query_grad, 'mem', scatter_dimension=0, tiled=True)  55 us
    reduce_scatter x1, waiting for transfers between devices, local(): lax.psum_scatter(key_grad, 'mem', scatter_dimension=0, tiled=True)  54.7 us
  transfers between devices with their start and end apart: 14, of which 14 were waited for; matrix products, arithmetic and copies ran while one was open for 6% of the time, Pallas kernels for 0%

commit v1 on v0

--- a/solution.py
+++ b/solution.py
@@ -1,8 +1,10 @@
+import functools
 import math
 import jax
 import jax.numpy as jnp
 from jax import lax
 from jax.sharding import PartitionSpec as P
+from jax.lax import all_gather
 
 H = 8
 HD = 128
@@ -11,6 +13,14 @@
 TOPK = 128
 EPSILON = 1e-05
 NEGATIVE = -1e30
+
+
+def manage_streams(local_block, bus_axis):
+    r2 = all_gather(local_block, bus_axis)
+    return jnp.sum(r2, axis=0)
+
+
+mix_vectors = functools.partial(manage_streams, bus_axis="mem")
 
 
 def outer_product(left, right):
@@ -159,7 +169,7 @@
     memory_high = lax.dynamic_update_slice_in_dim(memory_high, seg_high, start_block, 0)
     memory_sum = lax.dynamic_update_slice_in_dim(memory_sum, seg_sum, start_block, 0)
     row_high = lax.pmax(memory_high.astype(jnp.bfloat16), "mem").astype(memory_high.dtype)
-    row_sum = lax.psum(memory_sum * jnp.exp(memory_high - row_high), "mem")
+    row_sum = mix_vectors(memory_sum * jnp.exp(memory_high - row_high))
     log_total = row_high + jnp.log(row_sum)
 
     def memory_second(pieces):

time: 1470 us -> 1440 us (0.980)
  waiting for transfers between devices: 927 us -> 878 us
  blocking collectives: 49.1 us -> 72.4 us
    psum x1 -> x0, waiting for transfers between devices: 46.3 us -> none  [local(): row_sum = lax.psum(memory_sum * jnp.exp(memory_high - row_high), 'mem')]
    all_gather x0 -> x1, blocking collectives: none -> 22.8 us  [manage_streams(): r2 = all_gather(local_block, bus_axis)]
    unnamed x85 -> x87, local copies, waits for them, and re-layouts: 35.1 us -> 34.8 us
  transfers between devices with their start and end apart: 14 -> 13, of which waited for: 14 -> 13; matrix products, arithmetic and copies ran while one was open for 6% -> 6% of each run, Pallas kernels for 0% -> 0%
where the time goes in v1:
time: 1440 us; the launch traced here: 1430 us
  waiting for transfers between devices  878 us (61%)
  matrix products  251 us (17%)
  local copies, waits for them, and re-layouts  147 us (10%)
  blocking collectives  72.4 us (5%)
  other arithmetic  39.2 us (3%)
  loops' own time  22.9 us (2%)
  between operations  16.2 us (1%)
    psum x1, waiting for transfers between devices, local(): lax.psum((norm_part, query_part, key_part, value_part, out_part, ffn_gain...  192 us
    reduce_scatter x1, waiting for transfers between devices, local(): lax.psum_scatter(up_grad, 'mem', scatter_dimension=0, tiled=True)  90.3 us
    reduce_scatter x1, waiting for transfers between devices, local(): lax.psum_scatter(down_grad, 'mem', scatter_dimension=0, tiled=True)  90.3 us
    reduce_scatter x1, waiting for transfers between devices, local(): lax.psum_scatter(gate_grad, 'mem', scatter_dimension=0, tiled=True)  90.2 us
    reduce_scatter x1, waiting for transfers between devices, local(): lax.psum_scatter(numerators.reshape(all_rows, model_width), 'mem', scatte...  71.4 us
    reduce_scatter x1, waiting for transfers between devices, local(): lax.psum_scatter(key_grad, 'mem', scatter_dimension=0, tiled=True)  55.1 us
    reduce_scatter x1, waiting for transfers between devices, local(): lax.psum_scatter(value_grad, 'mem', scatter_dimension=0, tiled=True)  54.7 us
    reduce_scatter x1, waiting for transfers between devices, local(): lax.psum_scatter(query_grad, 'mem', scatter_dimension=0, tiled=True)  54.6 us
  transfers between devices with their start and end apart: 13, of which 13 were waited for; matrix products, arithmetic and copies ran while one was open for 6% of the time, Pallas kernels for 0%

profile of v1, /device:TPU:0, one launch (start us, length us, event | category | flops | bytes accessed | tf_op | source)
XLA Modules:
  0.0 1427.7 jit_solution(17964753101726673668)
XLA Ops:
  15.6 22.7 %while.110 = (s32[]{:T(128)}, bf16[4,128,1024]{2,1,0:T(8,128)(2,1)}, bf16[4,128,1024]{2,1,0:T(8,128)(2,1)}, s32[4,128]{1,0:T(4,128)S(1)}, pred[4,128]{1,0:T(4,12...) while((s32[]{:T(128)}, bf16[4,128,1024]{2,1,0:T(8,128)(2,1)}, ...), condition=%wide.region_2.3_spmd.clone, body=%wide.region_1.2_spmd.clone.sunk | while | flops 537657344 | bytes 4721261 | solution.py:124
  43.3 8.3 all-gather.4.cloned.1.call-done
  57.8 20.9 %while.111 = (s32[]{:T(128)}, f32[4,512,8]{1,2,0:T(8,128)S(1)}, f32[4,512,8]{1,2,0:T(8,128)S(1)}, s32[4]{0:T(128)S(1)}, pred[256]{0:T(512)(128)(4,1)S(1)}, /*ind...) while((s32[]{:T(128)}, f32[4,512,8]{1,2,0:T(8,128)S(1)}, ...), condition=%wide.region_10.11_spmd.clone, body=%wide.region_7.10_spmd.clone.sunk | while | flops 277078784 | bytes 10475995 | solution.py:165
  78.7 9.8 while.106
  88.6 23.5 %pmax.7 = bf16[4,512,8]{1,2,0:T(8,128)(2,1)S(1)} all-reduce(bf16[4,512,8]{1,2,0:T(8,128)(2,1)S(1)} %get-tuple-element.1010), channel_id=1, replica_groups=mesh['seg'=4,'mem'=8] {'mem'}, use_global_device_ids=true, to_apply=%region_11.12 | all-reduce | flops 16384 | bytes 65536 | tf_op jit(solution)/shard_map/pmax | solution.py:171
  112.1 22.8 %all-gather = f32[32,512,8]{1,2,0:T(8,128)} all-gather(f32[4,512,8]{1,2,0:T(8,128)S(1)} %fusion.205), channel_id=2, replica_groups=mesh['seg'=4,'mem'=8] {'mem'}, dimensions={0}, use_global_device_ids=true | all-gather | bytes 589824 | tf_op jit(solution)/shard_map/all_gather | solution.py:19
  136.1 4.3 broadcast.311.clone3.1
  140.3 26.2 %while.112 = (s32[]{:T(128)}, f32[4,512,8,128]{3,1,2,0:T(8,128)}, s32[4]{0:T(128)S(1)}, pred[256]{0:T(512)(128)(4,1)S(1)}, s32[]{:T(128)}, /*index=5*/bf16[4,512...) while((s32[]{:T(128)}, f32[4,512,8,128]{3,1,2,0:T(8,128)}, ...), condition=%wide.region_16.17_spmd.clone, body=%wide.region_15.16_spmd.clone.sunk | while | flops 542376704 | bytes 4643303 | solution.py:194
  142.4 4.5 bitcast_dynamic-update-slice_fusion.17
  149.0 4.4 bitcast_dynamic-update-slice_fusion.17
  155.5 4.5 bitcast_dynamic-update-slice_fusion.17
  162.0 4.5 bitcast_dynamic-update-slice_fusion.17
  170.7 46.0 %while.107 = (s32[]{:T(128)}, f32[4,512,8,128]{3,1,2,0:T(8,128)}, bf16[4,128,8,128]{3,2,1,0:T(8,128)(2,1)}, pred[4,128]{1,0:T(4,128)(4,1)S(1)}, bf16[4,128,8,128...) while((s32[]{:T(128)}, f32[4,512,8,128]{3,1,2,0:T(8,128)}, ...), condition=%wide.region_14.15_spmd, body=%wide.region_13.14_spmd.sunk | while | flops 271056896 | bytes 13158765 | solution.py:183
  216.7 10.3 add.248
  227.0 8.2 copy.98
  235.3 5.4 copy.151
  240.7 71.4 %reduce-scatter.10.cloned.1.call-done = f32[256,1024]{1,0:T(8,128)} async-done(((f32[2048,1024]{1,0:T(8,128)}), f32[256,1024]{1,0:T(8,128)}) %reduce-scatter.10.cloned.1.call-update) | async-done | bytes 1048592 | tf_op jit(solution)/shard_map/reduce_scatter | solution.py:195
  315.2 6.3 fusion.216
  324.8 5.9 multiply_convert_fusion
  340.3 34.3 %all-gather.6.cloned.1.call-done = bf16[2048,1024]{1,0:T(8,128)(2,1)} async-done(((bf16[256,1024]{1,0:T(8,128)(2,1)}), bf16[2048,1024]{1,0:T(8,128)(2,1)}) %all-gather.6.cloned.1.call-update) | async-done | bytes 4194320 | tf_op jit(solution)/shard_map/all_gather | solution.py:222
  380.8 28.1 %while.113 = (s32[]{:T(128)}, f32[4,512,8]{1,2,0:T(8,128)S(1)}, s32[4]{0:T(128)S(1)}, pred[256]{0:T(512)(128)(4,1)S(1)}, s32[]{:T(128)}, /*index=5*/bf16[4,512,8...) while((s32[]{:T(128)}, f32[4,512,8]{1,2,0:T(8,128)S(1)}, ...), condition=%wide.region_25.26_spmd.clone, body=%wide.region_23.25_spmd.clone.sunk | while | flops 543421184 | bytes 12032499 | solution.py:250
  408.9 15.7 %while.108 = (s32[]{:T(128)}, f32[4,512,8]{1,2,0:T(8,128)S(1)}, pred[4,128]{1,0:T(4,128)(4,1)S(1)}, bf16[4,128,8,128]{3,1,2,0:T(8,128)(2,1)}, bf16[4,512,8,128]{...) while((s32[]{:T(128)}, f32[4,512,8]{1,2,0:T(8,128)S(1)}, ...), condition=%wide.region_22.23_spmd, body=%wide.region_20.22_spmd.sunk | while | flops 271577088 | bytes 6917489 | solution.py:233
  425.3 52.5 %all-reduce.8.cloned.1.call-done = f32[4,512,8]{1,2,0:T(8,128)} async-done(((f32[4,512,8]{1,2,0:T(8,128)}), f32[4,512,8]{1,2,0:T(8,128)}) %all-reduce.8.cloned.1.call-update) | async-done | bytes 65552 | tf_op jit(solution)/shard_map/psum | solution.py:251
  482.1 55.5 %while.109 = (s32[]{:T(128)}, f32[4,512,8,128]{3,1,2,0:T(8,128)}, bf16[4,128,8,128]{3,1,2,0:T(8,128)(2,1)}, pred[4,128]{1,0:T(4,128)(4,1)S(1)}, bf16[4,512,8,128...) while((s32[]{:T(128)}, f32[4,512,8,128]{3,1,2,0:T(8,128)}, ...), condition=%wide.region_28.29_spmd, body=%wide.region_27.28_spmd.sunk | while | flops 407371776 | bytes 17665912 | solution.py:268
  485.6 4.6 multiply_bitcast_fusion.2
  499.5 4.6 multiply_bitcast_fusion.2
  513.2 4.6 multiply_bitcast_fusion.2
  527.0 4.6 multiply_bitcast_fusion.2
  541.9 50.4 %while.114 = (s32[]{:T(128)}, f32[256,8,128]{0,2,1:T(8,128)}, f32[256,8,128]{0,2,1:T(8,128)}, f32[4,512,8,128]{3,1,2,0:T(8,128)}, s32[4]{0:T(128)S(1)}, /*index=...) while((s32[]{:T(128)}, f32[256,8,128]{0,2,1:T(8,128)}, ...), condition=%wide.region_30.31_spmd.clone, body=%wide.region_29.30_spmd.clone.sunk | while | flops 1357906688 | bytes 65264296 | solution.py:305
  592.3 10.3 add.257
  602.6 8.2 copy.117
  610.9 5.4 copy.150
  616.3 4.4 fusion.199
  631.2 7.6 fusion.219
  638.9 7.5 fusion.218
  646.5 7.6 fusion.220
  654.2 33.0 %reduce-scatter.12.cloned.1.call-done = f32[256,1024]{1,0:T(8,128)} async-done(((f32[2048,1024]{1,0:T(8,128)}), f32[256,1024]{1,0:T(8,128)}) %reduce-scatter.12.cloned.1.call-update) | async-done | bytes 1048592 | tf_op jit(solution)/shard_map/reduce_scatter | solution.py:309
  691.2 50.8 %reduce-scatter.20.cloned.1.call-done = f32[128,1024]{1,0:T(8,128)} async-done(((f32[1024,1024]{1,0:T(8,128)}), f32[128,1024]{1,0:T(8,128)}) %reduce-scatter.20.cloned.1.call-update) | async-done | bytes 524304 | tf_op jit(solution)/shard_map/reduce_scatter | solution.py:327
  742.1 54.7 %reduce-scatter.18.cloned.1.call-done = f32[128,1024]{1,0:T(8,128)} async-done(((f32[1024,1024]{1,0:T(8,128)}), f32[128,1024]{1,0:T(8,128)}) %reduce-scatter.18.cloned.1.call-update) | async-done | bytes 524304 | tf_op jit(solution)/shard_map/reduce_scatter | solution.py:326
  796.7 55.1 %reduce-scatter.16.cloned.1.call-done = f32[128,1024]{1,0:T(8,128)} async-done(((f32[1024,1024]{1,0:T(8,128)}), f32[128,1024]{1,0:T(8,128)}) %reduce-scatter.16.cloned.1.call-update) | async-done | bytes 524304 | tf_op jit(solution)/shard_map/reduce_scatter | solution.py:325
  851.9 90.3 %reduce-scatter.24.cloned.1.call-done = f32[128,2816]{1,0:T(8,128)} async-done(((f32[1024,2816]{1,0:T(8,128)}), f32[128,2816]{1,0:T(8,128)}) %reduce-scatter.24.cloned.1.call-update) | async-done | bytes 1441808 | tf_op jit(solution)/shard_map/reduce_scatter | solution.py:330
  942.2 90.2 %reduce-scatter.22.cloned.1.call-done = f32[128,2816]{1,0:T(8,128)} async-done(((f32[1024,2816]{1,0:T(8,128)}), f32[128,2816]{1,0:T(8,128)}) %reduce-scatter.22.cloned.1.call-update) | async-done | bytes 1441808 | tf_op jit(solution)/shard_map/reduce_scatter | solution.py:329
  1032.4 90.3 %reduce-scatter.26.cloned.1.call-done = f32[352,1024]{1,0:T(8,128)} async-done(((f32[2816,1024]{1,0:T(8,128)}), f32[352,1024]{1,0:T(8,128)}) %reduce-scatter.26.cloned.1.call-update) | async-done | bytes 1441808 | tf_op jit(solution)/shard_map/reduce_scatter | solution.py:331
  1122.7 54.6 %reduce-scatter.14.cloned.1.call-done = f32[128,1024]{1,0:T(8,128)} async-done(((f32[1024,1024]{1,0:T(8,128)}), f32[128,1024]{1,0:T(8,128)}) %reduce-scatter.14.cloned.1.call-update) | async-done | bytes 524304 | tf_op jit(solution)/shard_map/reduce_scatter | solution.py:324
  1178.5 5.9 fusion.184
  1189.2 13.5 all-reduce.2
  1202.9 12.5 all-reduce.3
  1218.0 191.8 %all-reduce.10.cloned.1.call-done = (f32[128,1024]{1,0:T(8,128)}, f32[128,1024]{1,0:T(8,128)}, f32[128,1024]{1,0:T(8,128)}, f32[128,1024]{1,0:T(8,128)}, f32[128...) async-done(((f32[128,1024]{1,0:T(8,128)}, f32[128,1024]{1,0:T(8,128)}, f32[128,1024]{1,0:T(8,128)}, f32[128,1024]{1,0:T(8,128)}, f32[128,2816]{1,0:T(8,128)}, ...) | async-done | bytes 6422544 | tf_op jit(solution)/shard_map/psum | solution.py:344
  (430 shorter events, 305.1 us)
Async XLA Ops:
  7.2 5.8 copy-start
  7.2 5.7 copy-start.3
  7.2 5.7 copy-start.26
  7.2 44.4 %all-gather.4.cloned.1.call-start = ((), (), s32[]{:S(2)}) async-start(), calls=%async_computation.9 | async-start | bytes 4718592 | tf_op jit(solution)/shard_map/all_gather | solution.py:125
  8.6 6.0 copy-start.28
  12.0 300.1 %reduce-scatter.10.cloned.1.call-start = ((), (), s32[]{:S(2)}) async-start(), calls=%async_computation.10 | async-start | bytes 9437184 | tf_op jit(solution)/shard_map/reduce_scatter | solution.py:195
  12.1 2.5 copy-start.14
  13.0 2.6 copy-start.31
  15.6 25.2 %copy-start.33 = (s32[256]{0:T(256)S(1)}, s32[256]{0:T(256)}, u32[]{:S(2)}) copy-start(s32[256]{0:T(256)} %param.35) | copy-start | bytes 3076
  240.6 74.4 %copy-start.30 = (f32[1024]{0:T(1024)S(1)}, f32[1024]{0:T(1024)}, u32[]{:S(2)}) copy-start(f32[1024]{0:T(1024)} %param.45) | copy-start | bytes 12292
  240.7 133.9 %all-gather.6.cloned.1.call-start = ((), (), s32[]{:S(2)}) async-start(), calls=%async_computation.11 | async-start | bytes 4718592 | tf_op jit(solution)/shard_map/all_gather | solution.py:222
  312.1 9.4 slice-start
  315.0 19.9 %copy-start.6 = (f32[256,1024]{1,0:T(8,128)}, f32[256,1024]{1,0:T(8,128)S(1)}, u32[]{:S(2)}) copy-start(f32[256,1024]{1,0:T(8,128)S(1)} %get-tuple-element.1028) | copy-start | bytes 3145732
  315.2 6.3 copy-start.10
  315.2 6.3 slice-start.1
  315.2 9.6 slice-start.4
  321.5 3.3 copy-start.16
  321.5 3.3 slice-start.5
  321.5 10.9 slice-start.2
  324.8 7.7 slice-start.3
  332.5 3.7 copy-start.7
  337.8 140.1 %all-reduce.8.cloned.1.call-start = ((), (), s32[]{:S(2)}) async-start(), calls=%async_computation.12 | async-start | bytes 131072 | tf_op jit(solution)/shard_map/psum | solution.py:251
  377.9 2.9 copy-start.24
  425.3 261.8 %reduce-scatter.12.cloned.1.call-start = ((), (), s32[]{:S(2)}) async-start(), calls=%async_computation.13 | async-start | bytes 9437184 | tf_op jit(solution)/shard_map/reduce_scatter | solution.py:309
  477.9 4.2 copy-start.25
  543.8 2.5 copy-start.11
  543.8 2.8 copy-start.22
  556.3 2.5 copy-start.11
  556.3 2.8 copy-start.22
  568.8 2.5 copy-start.11
  568.8 2.8 copy-start.22
  581.4 2.5 copy-start.11
  581.4 2.8 copy-start.22
  616.3 125.8 %reduce-scatter.20.cloned.1.call-start = ((), (), s32[]{:S(2)}) async-start(), calls=%async_computation.17 | async-start | bytes 4718592 | tf_op jit(solution)/shard_map/reduce_scatter | solution.py:327
  620.7 176.0 %reduce-scatter.18.cloned.1.call-start = ((), (), s32[]{:S(2)}) async-start(), calls=%async_computation.16 | async-start | bytes 4718592 | tf_op jit(solution)/shard_map/reduce_scatter | solution.py:326
  625.6 226.2 %reduce-scatter.16.cloned.1.call-start = ((), (), s32[]{:S(2)}) async-start(), calls=%async_computation.15 | async-start | bytes 4718592 | tf_op jit(solution)/shard_map/reduce_scatter | solution.py:325
  631.0 311.2 %reduce-scatter.24.cloned.1.call-start = ((), (), s32[]{:S(2)}) async-start(), calls=%async_computation.19 | async-start | bytes 12976128 | tf_op jit(solution)/shard_map/reduce_scatter | solution.py:330
  638.9 393.5 %reduce-scatter.22.cloned.1.call-start = ((), (), s32[]{:S(2)}) async-start(), calls=%async_computation.18 | async-start | bytes 12976128 | tf_op jit(solution)/shard_map/reduce_scatter | solution.py:329
  646.4 476.3 %reduce-scatter.26.cloned.1.call-start = ((), (), s32[]{:S(2)}) async-start(), calls=%async_computation.20 | async-start | bytes 12976128 | tf_op jit(solution)/shard_map/reduce_scatter | solution.py:331
  654.1 523.1 %reduce-scatter.14.cloned.1.call-start = ((), (), s32[]{:S(2)}) async-start(), calls=%async_computation.14 | async-start | bytes 4718592 | tf_op jit(solution)/shard_map/reduce_scatter | solution.py:324
  691.2 486.1 %copy-start.34 = (u32[32]{0:T(128)S(1)}, u32[32]{0:T(128)}, u32[]{:S(2)}) copy-start(u32[32]{0:T(128)} %constant.261) | copy-start | bytes 388
  691.2 718.7 %all-reduce.10.cloned.1.call-start = ((), (), s32[]{:S(2)}) async-start(), calls=%async_computation.21 | async-start | bytes 12845056 | tf_op jit(solution)/shard_map/psum | solution.py:344
  1178.5 5.9 copy-start.12
  1178.5 5.9 copy-start.13
  1186.5 2.7 copy-start.32
  1409.9 7.8 copy-start.21
  1409.9 8.9 copy-start.20
  1411.9 8.0 copy-start.19
  (21 other events, 38.8 us)
Sparse Core Ops, SparseCore 0:
  12.1 39.4 all-gather.3
  240.8 71.2 reduce-scatter.9
  337.9 36.6 all-gather.5
  425.4 52.4 all-reduce.7
  616.4 70.6 reduce-scatter.11
  690.7 51.3 reduce-scatter.19
  745.4 51.2 reduce-scatter.17
  800.5 51.3 reduce-scatter.15
  855.4 86.7 reduce-scatter.23
  945.5 86.7 reduce-scatter.21
  1035.9 86.7 reduce-scatter.25
  1125.9 51.3 reduce-scatter.13
  1180.5 229.3 all-reduce.9
